TPU v7x, 512 devices: a whole 4x8x8 slice. The times are simulated.
512 devices in a mesh: rows: 32 (over y_lo, z, core), cols: 16 (over x, y_hi).
Axes of the slice: x: 4, y: 8 (y_hi: 4, y_lo: 2; y = y_hi * 2 + y_lo), z: 8, core: 2. Of those that a mesh axis runs over, the one named last changes fastest.
Arguments:
- pair_rep: bfloat16 [128, 4096, 128], P('rows', 'cols'), may hold values from -6 to 6
- project_weight: bfloat16 [128, 512], replicated, may hold values from -0.5 to 0.5
- output_weight: bfloat16 [128, 128], replicated, may hold values from -0.5 to 0.5
- pair_bias: bfloat16 [4, 4096, 4096], P(None, 'cols', 'rows'), may hold values from -4 to 300
- chain_valid: int32 [32], replicated, may hold values from 1 to 128, as said below
Outputs:
- update: bfloat16 [128, 4096, 128], P('rows', 'cols')
Inputs may be any that keep to these rules, and one draw needn't show every extreme that they name: Chain c occupies residues c * 128 to (c + 1) * 128 - 1; its first chain_valid[c] residues are valid; some chain is full.
All inputs are finite; a program needn't handle non-finite values.
Results may differ from a plain program's by a relative error of at most 0.0075.
Values may be sent and summed in bfloat16 or wider, within the bound.
No kernel may reach another device: no remote copies, remote signals or barrier semaphores. Data moves between devices by JAX's collectives and lax.ppermute only.
A program may use at most 64 MiB of HBM per device.

v0:
```python
import jax
import jax.numpy as jnp
from jax import lax
from jax.sharding import PartitionSpec as P

SLOT = 128


def attend(carry, query_head, key_piece, value_piece, bias_piece, chain_valid):
    count = key_piece.shape[2]
    position = jnp.arange(count, dtype=jnp.int32)
    chains = chain_valid.shape[0]
    member = (position // SLOT)[:, None] == jnp.arange(chains, dtype=jnp.int32)[None, :]
    allowed = jnp.sum(jnp.where(member, chain_valid[None, :], 0), axis=1)
    mask_add = jnp.where(position % SLOT < allowed, 0.0, -1000000000.0).astype(jnp.float32)
    block = 512

    def step(number, state):
        total, running_max, running_sum = state
        offset = number * block
        key_block = lax.dynamic_slice_in_dim(key_piece, offset, block, 2)
        value_block = lax.dynamic_slice_in_dim(value_piece, offset, block, 2)
        bias_block = lax.dynamic_slice_in_dim(bias_piece, offset, block, 1)
        mask_block = lax.dynamic_slice_in_dim(mask_add, offset, block, 0)
        scores = jnp.einsum(
            "rjd,rdk->rjk", query_head, key_block, preferred_element_type=jnp.float32
        )
        scores = scores + bias_block.astype(jnp.float32)[None] + mask_block[None, None, :]
        new_max = jnp.maximum(running_max, jnp.max(scores, axis=2))
        rescale = jnp.exp(running_max - new_max)
        weights = jnp.exp(scores - new_max[:, :, None])
        running_sum = running_sum * rescale + jnp.sum(weights, axis=2)
        weighted = jnp.einsum(
            "rdk,rjk->rdj",
            value_block,
            weights.astype(jnp.bfloat16),
            preferred_element_type=jnp.float32,
        )
        total = total * rescale[:, None, :] + weighted
        return (total, new_max, running_sum)

    return lax.fori_loop(0, count // block, step, carry)


def local(pair_rep, project_weight, output_weight, pair_bias, chain_valid):
    rows_here, cols_here, width = pair_rep.shape
    heads = pair_bias.shape[0]
    inner = output_weight.shape[0]
    head_size = inner // heads
    pair_f = pair_rep.astype(jnp.float32)
    center = jnp.mean(pair_f, axis=-1, keepdims=True)
    spread = jnp.mean(jnp.square(pair_f - center), axis=-1, keepdims=True)
    normed = ((pair_f - center) * lax.rsqrt(spread + 1e-05)).astype(jnp.bfloat16)
    project = jnp.dot(
        normed.reshape(rows_here * cols_here, width),
        project_weight,
        preferred_element_type=jnp.float32,
    )
    queries = (project[:, :inner] * head_size ** (-0.5)).astype(jnp.bfloat16)
    queries = queries.reshape(rows_here, cols_here, heads, head_size).transpose(0, 2, 1, 3)
    key_part = project[:, inner : 2 * inner].astype(jnp.bfloat16)
    key_part = key_part.reshape(rows_here, cols_here, heads, head_size).transpose(0, 2, 3, 1)
    value_part = project[:, 2 * inner : 3 * inner].astype(jnp.bfloat16)
    value_part = value_part.reshape(rows_here, cols_here, heads, head_size).transpose(0, 2, 3, 1)
    gate = jax.nn.sigmoid(project[:, 3 * inner :])
    outputs = []
    for head_index in range(heads):
        query_head = queries[:, head_index]
        key_head = key_part[:, head_index]
        value_head = value_part[:, head_index]
        bias_head = pair_bias[head_index]
        start_state = (
            jnp.zeros((rows_here, head_size, cols_here), jnp.float32),
            jnp.full((rows_here, cols_here), -jnp.inf, jnp.float32),
            jnp.zeros((rows_here, cols_here), jnp.float32),
        )
        bias_row = lax.all_gather(bias_head, "rows", axis=1, tiled=True)
        state = attend(
            start_state,
            query_head,
            lax.all_gather(key_head, "cols", axis=2, tiled=True),
            lax.all_gather(value_head, "cols", axis=2, tiled=True),
            bias_row,
            chain_valid,
        )
        total, running_max, running_sum = state
        outputs.append(total / running_sum[:, None, :])
    stacked = jnp.stack(outputs, axis=1).transpose(0, 3, 1, 2).reshape(rows_here * cols_here, inner)
    gated = (stacked * gate).astype(jnp.bfloat16)
    update = jnp.dot(gated, output_weight, preferred_element_type=jnp.float32).astype(jnp.bfloat16)
    return update.reshape(rows_here, cols_here, width)


def solution(mesh):
    return jax.shard_map(
        local,
        mesh=mesh,
        in_specs=(P("rows", "cols", None), P(), P(), P(None, "cols", "rows"), P()),
        out_specs=P("rows", "cols", None),
        check_vma=False,
    )
```

profile of v0, /device:TPU:1, one launch (start us, length us, event | category | flops | bytes accessed | tf_op | source)
XLA Modules:
  0.0 814.8 jit_solution(14056148589035336416)
XLA Ops:
  6.5 1.1 convert_reduce_fusion
  7.7 1.3 fusion.34
  9.0 1.3 fusion.35
  21.5 53.6 %all-gather.25.cloned.1.call-done = bf16[4,1,32,4096]{3,0,2,1:T(4,128)(2,1)} async-done(((bf16[4,1,32,256]{3,0,2,1:T(4,128)(2,1)}), bf16[4,1,32,4096]{3,0,2,1:T(4,128)(2,1)}) %all-gather.25.cloned.1.call-update) | async-done | bytes 1048592 | tf_op jit(solution)/shard_map/all_gather | solution.py:81
  75.2 60.8 %all-gather.29.cloned.1.call-done = bf16[4,1,32,4096]{3,0,2,1:T(4,128)(2,1)} async-done(((bf16[4,1,32,256]{3,0,2,1:T(4,128)(2,1)}), bf16[4,1,32,4096]{3,0,2,1:T(4,128)(2,1)}) %all-gather.29.cloned.1.call-update) | async-done | bytes 1048592 | tf_op jit(solution)/shard_map/all_gather | solution.py:82
  135.9 70.5 %all-gather.27.cloned.1.call-done = bf16[1,256,4096]{1,2,0:T(8,128)(2,1)} async-done(((bf16[1,256,128]{1,2,0:T(8,128)(2,1)}), bf16[1,256,4096]{1,2,0:T(8,128)(2,1)}) %all-gather.27.cloned.1.call-update) | async-done | bytes 2097168 | tf_op jit(solution)/shard_map/all_gather | solution.py:77
  206.4 27.7 %while.72 = (s32[]{:T(128)}, f32[4,32,256]{2,1,0:T(8,128)S(1)}, f32[4,256]{1,0:T(4,128)S(1)}, f32[4,256]{1,0:T(4,128)S(1)}, bf16[4,32,4096]{2,0,1:T(4,128)(2,1)}...) while((s32[]{:T(128)}, f32[4,32,256]{2,1,0:T(8,128)S(1)}, ...), condition=%wide.region_6.7_spmd.clone, body=%wide.region_3.6_spmd.clone.sunk | while | flops 71013376 | bytes 8788163 | solution.py:42
  209.9 1.1 constant_dynamic-slice_fusion.12
  213.3 1.1 constant_dynamic-slice_fusion.12
  216.8 1.1 constant_dynamic-slice_fusion.12
  220.3 1.1 constant_dynamic-slice_fusion.12
  223.7 1.1 constant_dynamic-slice_fusion.12
  227.2 1.1 constant_dynamic-slice_fusion.12
  230.7 1.1 constant_dynamic-slice_fusion.12
  234.1 31.4 %all-gather.35.cloned.1.call-done = bf16[4,1,32,4096]{3,0,2,1:T(4,128)(2,1)} async-done(((bf16[4,1,32,256]{3,0,2,1:T(4,128)(2,1)}), bf16[4,1,32,4096]{3,0,2,1:T(4,128)(2,1)}) %all-gather.35.cloned.1.call-update) | async-done | bytes 1048592 | tf_op jit(solution)/shard_map/all_gather | solution.py:82
  265.6 60.6 %all-gather.31.cloned.1.call-done = bf16[4,1,32,4096]{3,0,2,1:T(4,128)(2,1)} async-done(((bf16[4,1,32,256]{3,0,2,1:T(4,128)(2,1)}), bf16[4,1,32,4096]{3,0,2,1:T(4,128)(2,1)}) %all-gather.31.cloned.1.call-update) | async-done | bytes 1048592 | tf_op jit(solution)/shard_map/all_gather | solution.py:81
  326.2 70.3 %all-gather.33.cloned.1.call-done = bf16[1,256,4096]{1,2,0:T(8,128)(2,1)} async-done(((bf16[1,256,128]{1,2,0:T(8,128)(2,1)}), bf16[1,256,4096]{1,2,0:T(8,128)(2,1)}) %all-gather.33.cloned.1.call-update) | async-done | bytes 2097168 | tf_op jit(solution)/shard_map/all_gather | solution.py:77
  396.5 27.7 %while.73 = (s32[]{:T(128)}, f32[4,32,256]{2,1,0:T(8,128)S(1)}, f32[4,256]{1,0:T(4,128)S(1)}, f32[4,256]{1,0:T(4,128)S(1)}, bf16[4,32,4096]{2,0,1:T(4,128)(2,1)}...) while((s32[]{:T(128)}, f32[4,32,256]{2,1,0:T(8,128)S(1)}, ...), condition=%wide.region_10.11_spmd.clone, body=%wide.region_7.10_spmd.clone.sunk | while | flops 71013376 | bytes 8788163 | solution.py:42
  400.0 1.1 constant_dynamic-slice_fusion.13
  403.5 1.1 constant_dynamic-slice_fusion.13
  406.9 1.1 constant_dynamic-slice_fusion.13
  410.4 1.1 constant_dynamic-slice_fusion.13
  413.9 1.1 constant_dynamic-slice_fusion.13
  417.3 1.1 constant_dynamic-slice_fusion.13
  420.8 1.1 constant_dynamic-slice_fusion.13
  424.2 31.6 %all-gather.37.cloned.1.call-done = bf16[4,1,32,4096]{3,0,2,1:T(4,128)(2,1)} async-done(((bf16[4,1,32,256]{3,0,2,1:T(4,128)(2,1)}), bf16[4,1,32,4096]{3,0,2,1:T(4,128)(2,1)}) %all-gather.37.cloned.1.call-update) | async-done | bytes 1048592 | tf_op jit(solution)/shard_map/all_gather | solution.py:81
  455.9 60.8 %all-gather.41.cloned.1.call-done = bf16[4,1,32,4096]{3,0,2,1:T(4,128)(2,1)} async-done(((bf16[4,1,32,256]{3,0,2,1:T(4,128)(2,1)}), bf16[4,1,32,4096]{3,0,2,1:T(4,128)(2,1)}) %all-gather.41.cloned.1.call-update) | async-done | bytes 1048592 | tf_op jit(solution)/shard_map/all_gather | solution.py:82
  516.7 70.5 %all-gather.39.cloned.1.call-done = bf16[1,256,4096]{1,2,0:T(8,128)(2,1)} async-done(((bf16[1,256,128]{1,2,0:T(8,128)(2,1)}), bf16[1,256,4096]{1,2,0:T(8,128)(2,1)}) %all-gather.39.cloned.1.call-update) | async-done | bytes 2097168 | tf_op jit(solution)/shard_map/all_gather | solution.py:77
  587.1 27.7 %while.74 = (s32[]{:T(128)}, f32[4,32,256]{2,1,0:T(8,128)S(1)}, f32[4,256]{1,0:T(4,128)S(1)}, f32[4,256]{1,0:T(4,128)S(1)}, bf16[4,32,4096]{2,0,1:T(4,128)(2,1)}...) while((s32[]{:T(128)}, f32[4,32,256]{2,1,0:T(8,128)S(1)}, ...), condition=%wide.region_14.15_spmd.clone, body=%wide.region_11.14_spmd.clone.sunk | while | flops 71013376 | bytes 8788163 | solution.py:42
  590.6 1.1 constant_dynamic-slice_fusion.14
  594.0 1.1 constant_dynamic-slice_fusion.14
  597.5 1.1 constant_dynamic-slice_fusion.14
  601.0 1.1 constant_dynamic-slice_fusion.14
  604.4 1.1 constant_dynamic-slice_fusion.14
  607.9 1.1 constant_dynamic-slice_fusion.14
  611.4 1.1 constant_dynamic-slice_fusion.14
  614.8 31.5 %all-gather.43.cloned.1.call-done = bf16[4,1,32,4096]{3,0,2,1:T(4,128)(2,1)} async-done(((bf16[4,1,32,256]{3,0,2,1:T(4,128)(2,1)}), bf16[4,1,32,4096]{3,0,2,1:T(4,128)(2,1)}) %all-gather.43.cloned.1.call-update) | async-done | bytes 1048592 | tf_op jit(solution)/shard_map/all_gather | solution.py:81
  646.3 60.8 %all-gather.47.cloned.1.call-done = bf16[4,1,32,4096]{3,0,2,1:T(4,128)(2,1)} async-done(((bf16[4,1,32,256]{3,0,2,1:T(4,128)(2,1)}), bf16[4,1,32,4096]{3,0,2,1:T(4,128)(2,1)}) %all-gather.47.cloned.1.call-update) | async-done | bytes 1048592 | tf_op jit(solution)/shard_map/all_gather | solution.py:82
  707.1 70.3 %all-gather.45.cloned.1.call-done = bf16[1,256,4096]{1,2,0:T(8,128)(2,1)} async-done(((bf16[1,256,128]{1,2,0:T(8,128)(2,1)}), bf16[1,256,4096]{1,2,0:T(8,128)(2,1)}) %all-gather.45.cloned.1.call-update) | async-done | bytes 2097168 | tf_op jit(solution)/shard_map/all_gather | solution.py:77
  777.4 27.7 %while.75 = (s32[]{:T(128)}, f32[4,32,256]{2,1,0:T(8,128)S(1)}, f32[4,256]{1,0:T(4,128)S(1)}, f32[4,256]{1,0:T(4,128)S(1)}, bf16[4,32,4096]{2,0,1:T(4,128)(2,1)}...) while((s32[]{:T(128)}, f32[4,32,256]{2,1,0:T(8,128)S(1)}, ...), condition=%wide.region_18.19_spmd.clone, body=%wide.region_15.18_spmd.clone.sunk | while | flops 71013376 | bytes 8788163 | solution.py:42
  780.9 1.1 constant_dynamic-slice_fusion.15
  784.4 1.1 constant_dynamic-slice_fusion.15
  787.8 1.1 constant_dynamic-slice_fusion.15
  791.3 1.1 constant_dynamic-slice_fusion.15
  794.8 1.1 constant_dynamic-slice_fusion.15
  798.2 1.1 constant_dynamic-slice_fusion.15
  801.7 1.1 constant_dynamic-slice_fusion.15
  806.0 2.0 convolution_convert_fusion
  (338 shorter events, 90.6 us)
Async XLA Ops:
  6.5 3.8 copy-start
  6.5 68.6 %all-gather.25.cloned.1.call-start = ((), (), s32[]{:S(2)}) async-start(), calls=%async_computation | async-start | bytes 1114112 | tf_op jit(solution)/shard_map/all_gather | solution.py:81
  10.8 10.0 %copy-start.1 = (f32[1024,512]{1,0:T(8,128)}, f32[1024,512]{1,0:T(8,128)S(1)}, u32[]{:S(2)}) copy-start(f32[1024,512]{1,0:T(8,128)S(1)} %get-tuple-element.940) | copy-start | bytes 6291460
  10.8 2.6 copy-start.2
  12.1 123.8 %all-gather.29.cloned.1.call-start = ((), (), s32[]{:S(2)}) async-start(), calls=%async_computation.2 | async-start | bytes 1114112 | tf_op jit(solution)/shard_map/all_gather | solution.py:82
  13.3 8.0 copy-start.3
  13.3 193.1 %all-gather.27.cloned.1.call-start = ((), (), s32[]{:S(2)}) async-start(), calls=%async_computation.1 | async-start | bytes 2162688 | tf_op jit(solution)/shard_map/all_gather | solution.py:77
  14.2 251.4 %all-gather.35.cloned.1.call-start = ((), (), s32[]{:S(2)}) async-start(), calls=%async_computation.5 | async-start | bytes 1114112 | tf_op jit(solution)/shard_map/all_gather | solution.py:82
  14.8 311.4 %all-gather.31.cloned.1.call-start = ((), (), s32[]{:S(2)}) async-start(), calls=%async_computation.3 | async-start | bytes 1114112 | tf_op jit(solution)/shard_map/all_gather | solution.py:81
  15.4 381.2 %all-gather.33.cloned.1.call-start = ((), (), s32[]{:S(2)}) async-start(), calls=%async_computation.4 | async-start | bytes 2162688 | tf_op jit(solution)/shard_map/all_gather | solution.py:77
  16.2 439.7 %all-gather.37.cloned.1.call-start = ((), (), s32[]{:S(2)}) async-start(), calls=%async_computation.6 | async-start | bytes 1114112 | tf_op jit(solution)/shard_map/all_gather | solution.py:81
  16.9 499.7 %all-gather.41.cloned.1.call-start = ((), (), s32[]{:S(2)}) async-start(), calls=%async_computation.8 | async-start | bytes 1114112 | tf_op jit(solution)/shard_map/all_gather | solution.py:82
  17.7 569.5 %all-gather.39.cloned.1.call-start = ((), (), s32[]{:S(2)}) async-start(), calls=%async_computation.7 | async-start | bytes 2162688 | tf_op jit(solution)/shard_map/all_gather | solution.py:77
  18.5 627.8 %all-gather.43.cloned.1.call-start = ((), (), s32[]{:S(2)}) async-start(), calls=%async_computation.9 | async-start | bytes 1114112 | tf_op jit(solution)/shard_map/all_gather | solution.py:81
  19.1 688.0 %all-gather.47.cloned.1.call-start = ((), (), s32[]{:S(2)}) async-start(), calls=%async_computation.11 | async-start | bytes 1114112 | tf_op jit(solution)/shard_map/all_gather | solution.py:82
  19.8 757.6 %all-gather.45.cloned.1.call-start = ((), (), s32[]{:S(2)}) async-start(), calls=%async_computation.10 | async-start | bytes 2162688 | tf_op jit(solution)/shard_map/all_gather | solution.py:77
  805.2 0.8 copy-start.4
Sparse Core Ops, SparseCore 0:
  12.3 62.8 all-gather.24
  78.1 57.7 all-gather.28
  138.1 68.2 all-gather.26
  209.3 56.2 all-gather.34
  268.4 57.7 all-gather.30
  328.2 68.2 all-gather.32
  399.5 56.3 all-gather.36
  458.9 57.7 all-gather.40
  518.8 68.2 all-gather.38
  590.0 56.2 all-gather.42
  649.3 57.7 all-gather.46
  709.1 68.2 all-gather.44
where the time goes:
time: 817 us; the launch traced here: 815 us
  waiting for transfers between devices  677 us (83%)
  other arithmetic  46.2 us (6%)
  local copies, waits for them, and re-layouts  43.4 us (5%)
  matrix products  32.4 us (4%)
  between operations  13.9 us (2%)
    all_gather x4, waiting for transfers between devices, local(): bias_row = lax.all_gather(bias_head, 'rows', axis=1, tiled=True)  282 us
    all_gather x4, waiting for transfers between devices, local(): lax.all_gather(value_head, 'cols', axis=2, tiled=True)  214 us
    all_gather x4, waiting for transfers between devices, local(): lax.all_gather(key_head, 'cols', axis=2, tiled=True)  177 us
    dynamic_slice x32, local copies, waits for them, and re-layouts, step(): value_block = lax.dynamic_slice_in_dim(value_piece, offset, block, 2)  34.1 us
    convert_element_type x32, other arithmetic, step(): bias_block.astype(jnp.float32)[None]  31.8 us
    dot_general x32, matrix products, step(): jnp.einsum('rjd,rdk->rjk', query_head, key_block, preferred_element_type=...  16.6 us
  transfers between devices with their start and end apart: 12, of which 12 were waited for; matrix products, arithmetic and copies ran while one was open for 11% of the time, Pallas kernels for 0%

commit v1 on v0

--- a/solution.py
+++ b/solution.py
@@ -74,7 +74,9 @@
             jnp.full((rows_here, cols_here), -jnp.inf, jnp.float32),
             jnp.zeros((rows_here, cols_here), jnp.float32),
         )
-        bias_row = lax.all_gather(bias_head, "rows", axis=1, tiled=True)
+        bias_row = jnp.concatenate(
+            lax.all_to_all(jnp.stack([bias_head] * lax.axis_size("rows")), "rows", 0, 0), axis=1
+        )
         state = attend(
             start_state,
             query_head,

time: 817 us -> 552 us (0.68)
  waiting for transfers between devices: 677 us -> 368 us
  starting transfers between devices: 0.44 us -> 39.6 us
    all_gather x4 -> x0, waiting for transfers between devices: 282 us -> none  [local(): bias_row = lax.all_gather(bias_head, 'rows', axis=1, tiled=True)]
    all_gather x4, waiting for transfers between devices: 177 us -> 84.1 us  [local(): lax.all_gather(key_head, 'cols', axis=2, tiled=True)]
    all_to_all x0 -> x4, waiting for transfers between devices: none -> 49.5 us  [local(): lax.all_to_all(jnp.stack([bias_head] * lax.axis_size('rows')), 'rows', 0, 0)]
    all_to_all x0 -> x4, starting transfers between devices: none -> 39.3 us  [local(): lax.all_to_all(jnp.stack([bias_head] * lax.axis_size('rows')), 'rows', 0, 0)]
    all_gather x4, waiting for transfers between devices: 214 us -> 231 us  [local(): lax.all_gather(value_head, 'cols', axis=2, tiled=True)]
  transfers between devices with their start and end apart: 12 -> 12, of which waited for: 12 -> 8; matrix products, arithmetic and copies ran while one was open for 11% -> 16% of each run, Pallas kernels for 0% -> 0%
where the time goes in v1:
time: 552 us; the launch traced here: 550 us
  waiting for transfers between devices  368 us (67%)
  local copies, waits for them, and re-layouts  47.4 us (9%)
  other arithmetic  46.2 us (8%)
  starting transfers between devices  39.6 us (7%)
  matrix products  32.5 us (6%)
  between operations  14 us (3%)
    all_gather x4, waiting for transfers between devices, local(): lax.all_gather(value_head, 'cols', axis=2, tiled=True)  231 us
    all_gather x4, waiting for transfers between devices, local(): lax.all_gather(key_head, 'cols', axis=2, tiled=True)  84.1 us
    all_to_all x4, waiting for transfers between devices, local(): lax.all_to_all(jnp.stack([bias_head] * lax.axis_size('rows')), 'rows', 0, 0)  49.5 us
    all_to_all x4, starting transfers between devices, local(): lax.all_to_all(jnp.stack([bias_head] * lax.axis_size('rows')), 'rows', 0, 0)  39.3 us
    dynamic_slice x32, local copies, waits for them, and re-layouts, step(): value_block = lax.dynamic_slice_in_dim(value_piece, offset, block, 2)  34.1 us
    convert_element_type x32, other arithmetic, step(): bias_block.astype(jnp.float32)[None]  31.8 us
    dot_general x32, matrix products, step(): jnp.einsum('rjd,rdk->rjk', query_head, key_block, preferred_element_type=...  16.7 us
    dot_general x32, matrix products, step(): jnp.einsum('rdk,rjk->rdj', value_block, weights.astype(jnp.bfloat16), pre...  13.4 us
  transfers between devices with their start and end apart: 12, of which 8 were waited for; matrix products, arithmetic and copies ran while one was open for 16% of the time, Pallas kernels for 0%

profile of v1, /device:TPU:1, one launch (start us, length us, event | category | flops | bytes accessed | tf_op | source)
XLA Modules:
  0.0 549.6 jit_solution(4339789104742517282)
XLA Ops:
  6.5 1.1 convert_reduce_fusion
  7.7 1.3 fusion.34
  9.0 1.3 fusion.35
  16.0 1.6 stack.27
  17.6 13.0 %all-to-all-start = ((bf16[32,256,128]{1,2,0:T(8,128)(2,1)}), bf16[32,256,128]{1,2,0:T(8,128)(2,1)}, u32[]{:S(2)}, u32[]{:S(2)}) async-start(bf16[32,256,128]{1,2,0:T(8,128)(2,1)} %stack.27), calls=%async_computation | async-start | bytes 4194304 | tf_op jit(solution)/shard_map/all_to_all | solution.py:78
  33.4 49.5 %all-to-all-done = bf16[32,256,128]{1,2,0:T(8,128)(2,1)} async-done(((bf16[32,256,128]{1,2,0:T(8,128)(2,1)}), bf16[32,256,128]{1,2,0:T(8,128)(2,1)}, u32[]{:S(2)}, u32[]{:S(2)}) %all-to-all-start) | async-done | bytes 2097184 | tf_op jit(solution)/shard_map/all_to_all | solution.py:78
  82.9 1.6 stack.29
  84.6 5.5 %all-to-all-start.1 = ((bf16[32,256,128]{1,2,0:T(8,128)(2,1)}), bf16[32,256,128]{1,2,0:T(8,128)(2,1)}, u32[]{:S(2)}, u32[]{:S(2)}) async-start(bf16[32,256,128]{1,2,0:T(8,128)(2,1)} %stack.29), calls=%async_computation.1 | async-start | bytes 4194304 | tf_op jit(solution)/shard_map/all_to_all | solution.py:78
  90.2 49.7 %all-gather.19.cloned.1.call-done = bf16[4,1,32,4096]{3,0,2,1:T(4,128)(2,1)} async-done(((bf16[4,1,32,256]{3,0,2,1:T(4,128)(2,1)}), bf16[4,1,32,4096]{3,0,2,1:T(4,128)(2,1)}) %all-gather.19.cloned.1.call-update) | async-done | bytes 1048592 | tf_op jit(solution)/shard_map/all_gather | solution.py:84
  139.9 27.7 %while.72 = (s32[]{:T(128)}, f32[4,32,256]{2,1,0:T(8,128)S(1)}, f32[4,256]{1,0:T(4,128)S(1)}, f32[4,256]{1,0:T(4,128)S(1)}, bf16[4,32,4096]{2,0,1:T(4,128)(2,1)}...) while((s32[]{:T(128)}, f32[4,32,256]{2,1,0:T(8,128)S(1)}, ...), condition=%wide.region_6.7_spmd.clone, body=%wide.region_3.6_spmd.clone.sunk | while | flops 71013376 | bytes 8788163 | solution.py:42
  143.3 1.1 constant_dynamic-slice_fusion.12
  146.8 1.1 constant_dynamic-slice_fusion.12
  150.3 1.1 constant_dynamic-slice_fusion.12
  153.7 1.1 constant_dynamic-slice_fusion.12
  157.2 1.1 constant_dynamic-slice_fusion.12
  160.7 1.1 constant_dynamic-slice_fusion.12
  164.1 1.1 constant_dynamic-slice_fusion.12
  167.6 1.6 stack.31
  169.3 10.3 %all-to-all-start.2 = ((bf16[32,256,128]{1,2,0:T(8,128)(2,1)}), bf16[32,256,128]{1,2,0:T(8,128)(2,1)}, u32[]{:S(2)}, u32[]{:S(2)}) async-start(bf16[32,256,128]{1,2,0:T(8,128)(2,1)} %stack.31), calls=%async_computation.2 | async-start | bytes 4194304 | tf_op jit(solution)/shard_map/all_to_all | solution.py:78
  179.6 25.6 %all-gather.21.cloned.1.call-done = bf16[4,1,32,4096]{3,0,2,1:T(4,128)(2,1)} async-done(((bf16[4,1,32,256]{3,0,2,1:T(4,128)(2,1)}), bf16[4,1,32,4096]{3,0,2,1:T(4,128)(2,1)}) %all-gather.21.cloned.1.call-update) | async-done | bytes 1048592 | tf_op jit(solution)/shard_map/all_gather | solution.py:83
  205.2 60.2 %all-gather.23.cloned.1.call-done = bf16[4,1,32,4096]{3,0,2,1:T(4,128)(2,1)} async-done(((bf16[4,1,32,256]{3,0,2,1:T(4,128)(2,1)}), bf16[4,1,32,4096]{3,0,2,1:T(4,128)(2,1)}) %all-gather.23.cloned.1.call-update) | async-done | bytes 1048592 | tf_op jit(solution)/shard_map/all_gather | solution.py:84
  265.4 27.7 %while.73 = (s32[]{:T(128)}, f32[4,32,256]{2,1,0:T(8,128)S(1)}, f32[4,256]{1,0:T(4,128)S(1)}, f32[4,256]{1,0:T(4,128)S(1)}, bf16[4,32,4096]{2,0,1:T(4,128)(2,1)}...) while((s32[]{:T(128)}, f32[4,32,256]{2,1,0:T(8,128)S(1)}, ...), condition=%wide.region_10.11_spmd.clone, body=%wide.region_7.10_spmd.clone.sunk | while | flops 71013376 | bytes 8788163 | solution.py:42
  268.8 1.1 constant_dynamic-slice_fusion.13
  272.3 1.1 constant_dynamic-slice_fusion.13
  275.8 1.1 constant_dynamic-slice_fusion.13
  279.2 1.1 constant_dynamic-slice_fusion.13
  282.7 1.1 constant_dynamic-slice_fusion.13
  286.2 1.1 constant_dynamic-slice_fusion.13
  289.6 1.1 constant_dynamic-slice_fusion.13
  293.1 1.6 stack.33
  294.7 10.4 %all-to-all-start.3 = ((bf16[32,256,128]{1,2,0:T(8,128)(2,1)}), bf16[32,256,128]{1,2,0:T(8,128)(2,1)}, u32[]{:S(2)}, u32[]{:S(2)}) async-start(bf16[32,256,128]{1,2,0:T(8,128)(2,1)} %stack.33), calls=%async_computation.3 | async-start | bytes 4194304 | tf_op jit(solution)/shard_map/all_to_all | solution.py:78
  305.1 25.5 %all-gather.25.cloned.1.call-done = bf16[4,1,32,4096]{3,0,2,1:T(4,128)(2,1)} async-done(((bf16[4,1,32,256]{3,0,2,1:T(4,128)(2,1)}), bf16[4,1,32,4096]{3,0,2,1:T(4,128)(2,1)}) %all-gather.25.cloned.1.call-update) | async-done | bytes 1048592 | tf_op jit(solution)/shard_map/all_gather | solution.py:83
  330.6 60.2 %all-gather.27.cloned.1.call-done = bf16[4,1,32,4096]{3,0,2,1:T(4,128)(2,1)} async-done(((bf16[4,1,32,256]{3,0,2,1:T(4,128)(2,1)}), bf16[4,1,32,4096]{3,0,2,1:T(4,128)(2,1)}) %all-gather.27.cloned.1.call-update) | async-done | bytes 1048592 | tf_op jit(solution)/shard_map/all_gather | solution.py:84
  390.8 27.7 %while.74 = (s32[]{:T(128)}, f32[4,32,256]{2,1,0:T(8,128)S(1)}, f32[4,256]{1,0:T(4,128)S(1)}, f32[4,256]{1,0:T(4,128)S(1)}, bf16[4,32,4096]{2,0,1:T(4,128)(2,1)}...) while((s32[]{:T(128)}, f32[4,32,256]{2,1,0:T(8,128)S(1)}, ...), condition=%wide.region_14.15_spmd.clone, body=%wide.region_11.14_spmd.clone.sunk | while | flops 71013376 | bytes 8788163 | solution.py:42
  394.2 1.1 constant_dynamic-slice_fusion.14
  397.7 1.1 constant_dynamic-slice_fusion.14
  401.2 1.1 constant_dynamic-slice_fusion.14
  404.6 1.1 constant_dynamic-slice_fusion.14
  408.1 1.1 constant_dynamic-slice_fusion.14
  411.6 1.1 constant_dynamic-slice_fusion.14
  415.0 1.1 constant_dynamic-slice_fusion.14
  418.5 33.0 %all-gather.29.cloned.1.call-done = bf16[4,1,32,4096]{3,0,2,1:T(4,128)(2,1)} async-done(((bf16[4,1,32,256]{3,0,2,1:T(4,128)(2,1)}), bf16[4,1,32,4096]{3,0,2,1:T(4,128)(2,1)}) %all-gather.29.cloned.1.call-update) | async-done | bytes 1048592 | tf_op jit(solution)/shard_map/all_gather | solution.py:83
  451.5 60.8 %all-gather.31.cloned.1.call-done = bf16[4,1,32,4096]{3,0,2,1:T(4,128)(2,1)} async-done(((bf16[4,1,32,256]{3,0,2,1:T(4,128)(2,1)}), bf16[4,1,32,4096]{3,0,2,1:T(4,128)(2,1)}) %all-gather.31.cloned.1.call-update) | async-done | bytes 1048592 | tf_op jit(solution)/shard_map/all_gather | solution.py:84
  512.3 27.7 %while.75 = (s32[]{:T(128)}, f32[4,32,256]{2,1,0:T(8,128)S(1)}, f32[4,256]{1,0:T(4,128)S(1)}, f32[4,256]{1,0:T(4,128)S(1)}, bf16[4,32,4096]{2,0,1:T(4,128)(2,1)}...) while((s32[]{:T(128)}, f32[4,32,256]{2,1,0:T(8,128)S(1)}, ...), condition=%wide.region_18.19_spmd.clone, body=%wide.region_15.18_spmd.clone.sunk | while | flops 71013376 | bytes 8788163 | solution.py:42
  515.7 1.1 constant_dynamic-slice_fusion.15
  519.2 1.1 constant_dynamic-slice_fusion.15
  522.6 1.1 constant_dynamic-slice_fusion.15
  540.8 2.0 convolution_convert_fusion
  (338 shorter events, 92.1 us)
Async XLA Ops:
  6.5 3.8 copy-start
  6.5 83.6 %all-gather.17.cloned.1.call-start = ((), (), s32[]{:S(2)}) async-start(), calls=%async_computation.4 | async-start | bytes 1114112 | tf_op jit(solution)/shard_map/all_gather | solution.py:83
  10.7 21.5 %copy-start.1 = (f32[1024,512]{1,0:T(8,128)}, f32[1024,512]{1,0:T(8,128)S(1)}, u32[]{:S(2)}) copy-start(f32[1024,512]{1,0:T(8,128)S(1)} %get-tuple-element.940) | copy-start | bytes 6291460
  10.8 5.1 copy-start.2
  12.1 127.7 %all-gather.19.cloned.1.call-start = ((), (), s32[]{:S(2)}) async-start(), calls=%async_computation.5 | async-start | bytes 1114112 | tf_op jit(solution)/shard_map/all_gather | solution.py:84
  13.4 191.8 %all-gather.21.cloned.1.call-start = ((), (), s32[]{:S(2)}) async-start(), calls=%async_computation.6 | async-start | bytes 1114112 | tf_op jit(solution)/shard_map/all_gather | solution.py:83
  14.1 251.3 %all-gather.23.cloned.1.call-start = ((), (), s32[]{:S(2)}) async-start(), calls=%async_computation.7 | async-start | bytes 1114112 | tf_op jit(solution)/shard_map/all_gather | solution.py:84
  14.7 315.9 %all-gather.25.cloned.1.call-start = ((), (), s32[]{:S(2)}) async-start(), calls=%async_computation.8 | async-start | bytes 1114112 | tf_op jit(solution)/shard_map/all_gather | solution.py:83
  15.3 375.5 %all-gather.27.cloned.1.call-start = ((), (), s32[]{:S(2)}) async-start(), calls=%async_computation.9 | async-start | bytes 1114112 | tf_op jit(solution)/shard_map/all_gather | solution.py:84
  17.6 65.3 %all-to-all-start = ((bf16[32,256,128]{1,2,0:T(8,128)(2,1)}), bf16[32,256,128]{1,2,0:T(8,128)(2,1)}, u32[]{:S(2)}, u32[]{:S(2)}) async-start(bf16[32,256,128]{1,2,0:T(8,128)(2,1)} %stack.27), calls=%async_computation | async-start | bytes 4194304 | tf_op jit(solution)/shard_map/all_to_all | solution.py:78
  30.6 2.6 copy-start.3
  30.6 420.8 %all-gather.29.cloned.1.call-start = ((), (), s32[]{:S(2)}) async-start(), calls=%async_computation.10 | async-start | bytes 1114112 | tf_op jit(solution)/shard_map/all_gather | solution.py:83
  31.4 480.9 %all-gather.31.cloned.1.call-start = ((), (), s32[]{:S(2)}) async-start(), calls=%async_computation.11 | async-start | bytes 1114112 | tf_op jit(solution)/shard_map/all_gather | solution.py:84
  84.6 83.0 %all-to-all-start.1 = ((bf16[32,256,128]{1,2,0:T(8,128)(2,1)}), bf16[32,256,128]{1,2,0:T(8,128)(2,1)}, u32[]{:S(2)}, u32[]{:S(2)}) async-start(bf16[32,256,128]{1,2,0:T(8,128)(2,1)} %stack.29), calls=%async_computation.1 | async-start | bytes 4194304 | tf_op jit(solution)/shard_map/all_to_all | solution.py:78
  169.3 123.8 %all-to-all-start.2 = ((bf16[32,256,128]{1,2,0:T(8,128)(2,1)}), bf16[32,256,128]{1,2,0:T(8,128)(2,1)}, u32[]{:S(2)}, u32[]{:S(2)}) async-start(bf16[32,256,128]{1,2,0:T(8,128)(2,1)} %stack.31), calls=%async_computation.2 | async-start | bytes 4194304 | tf_op jit(solution)/shard_map/all_to_all | solution.py:78
  294.7 217.5 %all-to-all-start.3 = ((bf16[32,256,128]{1,2,0:T(8,128)(2,1)}), bf16[32,256,128]{1,2,0:T(8,128)(2,1)}, u32[]{:S(2)}, u32[]{:S(2)}) async-start(bf16[32,256,128]{1,2,0:T(8,128)(2,1)} %stack.33), calls=%async_computation.3 | async-start | bytes 4194304 | tf_op jit(solution)/shard_map/all_to_all | solution.py:78
  540.0 0.8 copy-start.4
Sparse Core Ops, SparseCore 0:
  12.3 65.4 all-gather.16
  80.8 59.0 all-gather.18
  142.9 62.2 all-gather.20
  208.0 57.2 all-gather.22
  268.2 62.3 all-gather.24
  333.5 57.2 all-gather.26
  393.7 57.6 all-gather.28
  454.5 57.7 all-gather.30
